TPU v7x, 32 devices: a whole 2x2x4 slice. The times are simulated.
32 devices in a mesh: dp: 4 (over y, x), mp: 8 (over z, core).
Axes of the slice: x: 2, y: 2, z: 4, core: 2. Of those that a mesh axis runs over, the one named last changes fastest.
Arguments:
- grads: bfloat16 [3, 8192, 28672], P(None, 'dp', 'mp'), may hold values from -8 to 8
- sketch: bfloat16 [28672, 256], P('mp'), may hold values from -0.03125 to 0.03125
- old_proj: bfloat16 [3, 8192, 256], P(None, 'dp'), may hold values from -0.0625 to 0.0625
- first_moment: float32 [3, 256, 28672], P(None, 'dp', 'mp'), may hold values from -12 to 12
- second_moment: float32 [3, 256, 28672], P(None, 'dp', 'mp'), may hold values from 0.25 to 4
- refresh_list: int32 [1], replicated, may hold values from 0 to 2
Outputs:
- new_first: float32 [3, 256, 28672], P(None, 'dp', 'mp')
- new_second: float32 [3, 256, 28672], P(None, 'dp', 'mp')
- direction: bfloat16 [3, 256, 28672], P(None, 'dp', 'mp')
All inputs are finite; a program needn't handle non-finite values.
Results may differ from a plain program's by a relative error of at most 0.0029.
Values sent between devices are 32-bit elements; how exact they have to be, the bound alone decides.
No kernel may reach another device: no remote copies, remote signals or barrier semaphores. Data moves between devices by JAX's collectives and lax.ppermute only.
A program may use at most 192 MiB of HBM per device.

v0:
```python
import jax
import jax.numpy as jnp
from jax import lax
from jax.sharding import PartitionSpec as P

first_decay = 0.9
second_decay = 0.95
epsilon = 1e-08
highest = lax.Precision.HIGHEST


def row_product(left, right):
    return lax.dot_general(
        left, right, (((0,), (0,)), ((), ())), precision=highest, preferred_element_type=jnp.float32
    )


def local(grads, sketch, old_proj, first_moment, second_moment, refresh_list):
    chosen = refresh_list[0]
    matrix_count = grads.shape[0]
    rank_rows = first_moment.shape[1]
    rank_total = sketch.shape[1]
    columns_total = sketch.shape[0] * lax.axis_size("mp")
    target = lax.dynamic_index_in_dim(grads, chosen, 0, keepdims=False)
    prior_proj = lax.dynamic_index_in_dim(old_proj, chosen, 0, keepdims=False).astype(jnp.float32)
    sketch_part = jnp.dot(target, sketch, preferred_element_type=jnp.float32)
    sketched = (lax.psum(sketch_part, "mp") / rank_total).astype(jnp.bfloat16)
    backward_part = lax.dot_general(
        target, sketched, (((0,), (0,)), ((), ())), preferred_element_type=jnp.float32
    )
    backward = (lax.psum(backward_part, "dp") / columns_total).astype(jnp.bfloat16)
    range_panel = lax.psum(jnp.dot(target, backward, preferred_element_type=jnp.float32), "mp")
    gram_part = row_product(range_panel, range_panel)
    gram_full = lax.psum(gram_part, "dp")
    factor = jnp.linalg.cholesky(gram_full)
    new_basis = jax.scipy.linalg.solve_triangular(factor, range_panel.T, lower=True).T
    turning = lax.psum(row_product(new_basis, prior_proj), "dp")
    picks = lax.broadcasted_iota(jnp.int32, (matrix_count, 1, 1), 0) == chosen
    projectors = jnp.where(picks, new_basis.astype(jnp.bfloat16)[None], old_proj)
    projected = jnp.transpose(
        lax.psum_scatter(
            jnp.einsum("kdr,kdc->rkc", projectors, grads, preferred_element_type=jnp.float32),
            "dp",
            scatter_dimension=0,
            tiled=True,
        ),
        (1, 0, 2),
    )
    first_own = lax.dynamic_index_in_dim(first_moment, chosen, 0, keepdims=False)
    second_own = lax.dynamic_index_in_dim(second_moment, chosen, 0, keepdims=False)
    own_start = lax.axis_index("dp") * rank_rows
    first_all, second_all = (
        lax.all_gather(first_own, "dp", axis=0, tiled=True),
        lax.all_gather(second_own, "dp", axis=0, tiled=True),
    )
    own_turning = lax.dynamic_slice_in_dim(turning, own_start, rank_rows, 0)
    turned_first = jnp.dot(own_turning, first_all, precision=highest)
    turned_second = jnp.dot(own_turning * own_turning, second_all, precision=highest)
    moved_first = jnp.where(picks, turned_first[None], first_moment)
    moved_second = jnp.where(picks, turned_second[None], second_moment)
    updated_first = first_decay * moved_first + (1.0 - first_decay) * projected
    updated_second = second_decay * moved_second + (1.0 - second_decay) * projected * projected
    direction = (updated_first / (jnp.sqrt(updated_second) + epsilon)).astype(jnp.bfloat16)
    return (updated_first, updated_second, direction)


def solution(mesh):
    placed = (
        P(None, "dp", "mp"),
        P("mp", None),
        P(None, "dp", None),
        P(None, "dp", "mp"),
        P(None, "dp", "mp"),
        P(),
    )
    return jax.shard_map(
        local,
        mesh=mesh,
        in_specs=placed,
        out_specs=(P(None, "dp", "mp"), P(None, "dp", "mp"), P(None, "dp", "mp")),
        check_vma=False,
    )
```

profile of v0, /device:TPU:0, one launch (start us, length us, event | category | flops | bytes accessed | tf_op | source)
XLA Modules:
  0.0 609.4 jit_solution(3067259670049275815)
XLA Ops:
  8.7 8.6 %fusion.4 = f32[2048,256]{1,0:T(8,128)} fusion(bf16[3584,256]{1,0:T(8,128)(2,1)S(1)} %copy-done, bf16[3,2048,3584]{2,1,0:T(8,128)(2,1)} %param.6, s32[]{:T(128)S(6)} %select_n.27), kind=kOutput, calls=%fused_computation.6 | convolution fusion | flops 3758096384 | bytes 18612228 | tf_op jit(solution)/shard_map/dot_general | solution.py:26
  17.3 68.0 %all-reduce.7.cloned.1.call-done = f32[2048,256]{1,0:T(8,128)} async-done(((f32[2048,256]{1,0:T(8,128)}), f32[2048,256]{1,0:T(8,128)}) %all-reduce.7.cloned.1.call-update) | async-done | bytes 2097168 | tf_op jit(solution)/shard_map/psum | solution.py:27
  85.3 11.6 %fusion.2 = f32[3584,256]{1,0:T(8,128)} fusion(bf16[3,2048,3584]{2,1,0:T(8,128)(2,1)} %param.6, s32[]{:T(128)S(6)} %select_n.27, f32[2048,256]{1,0:T(8,128)} %all-reduce.7.cloned.1.call-done), kind=kOutput, calls=%fused_computation.4 | convolution fusion | flops 3759144960 | bytes 20447236 | tf_op jit(solution)/shard_map/dot_general | solution.py:28
  97.0 95.4 %all-reduce.9.cloned.1.call-done = f32[3584,256]{1,0:T(8,128)} async-done(((f32[3584,256]{1,0:T(8,128)}), f32[3584,256]{1,0:T(8,128)}) %all-reduce.9.cloned.1.call-update) | async-done | bytes 3670032 | tf_op jit(solution)/shard_map/psum | solution.py:31
  192.4 11.5 %fusion = f32[2048,256]{1,0:T(8,128)} fusion(bf16[3,2048,3584]{2,1,0:T(8,128)(2,1)} %param.6, s32[]{:T(128)S(6)} %select_n.27, f32[3584,256]{1,0:T(8,128)} %all-reduce.9.cloned.1.call-done), kind=kOutput, calls=%fused_computation.2 | convolution fusion | flops 3759931392 | bytes 20447236 | tf_op jit(solution)/shard_map/dot_general | solution.py:32
  204.4 64.7 %all-reduce.11.cloned.1.call-done = f32[2048,256]{1,0:T(8,128)} async-done(((f32[2048,256]{1,0:T(8,128)}), f32[2048,256]{1,0:T(8,128)}) %all-reduce.11.cloned.1.call-update) | async-done | bytes 2097168 | tf_op jit(solution)/shard_map/psum | solution.py:32
  269.2 6.4 %fusion.48 = f32[256,256]{0,1:T(8,128)} fusion(f32[2048,256]{1,0:T(8,128)} %all-reduce.11.cloned.1.call-done), kind=kOutput, calls=%fused_computation.75 | convolution fusion | flops 1610612736 | bytes 2359296 | tf_op jit(solution)/shard_map/dot_general | solution.py:13
  275.6 2.2 constant_dynamic-slice_fusion.1
  277.9 40.5 %all-reduce.13.cloned.1.call-done = f32[256,256]{0,1:T(8,128)} async-done(((f32[256,256]{0,1:T(8,128)}), f32[256,256]{0,1:T(8,128)}) %all-reduce.13.cloned.1.call-update) | async-done | bytes 262160 | tf_op jit(solution)/shard_map/psum | solution.py:34
  320.5 11.7 %cholesky.50 = f32[128,128]{1,0:T(8,128)S(1)} custom-call(f32[128,128]{1,0:T(8,128)S(1)} %cholesky.118), custom_call_target="Cholesky" | custom-call | tf_op jit(solution)/shard_map/jit(cholesky)/cholesky | solution.py:35
  332.2 9.8 %custom-call.15 = f32[1,128,128]{1,2,0:T(8,128)S(1)} custom-call(f32[1,128,128]{2,1,0:T(8,128)S(1)} %get-tuple-element.27), custom_call_target="InvertDiagBlocksLowerTriangular" | custom-call | tf_op jit(solution)/shard_map/jit(cholesky)/cholesky | solution.py:35
  342.5 11.7 %cholesky.105 = f32[128,128]{1,0:T(8,128)S(1)} custom-call(f32[128,128]{1,0:T(8,128)S(1)} %convolution_subtract_fusion.1), custom_call_target="Cholesky" | custom-call | tf_op jit(solution)/shard_map/jit(cholesky)/cholesky | solution.py:35
  356.5 4.2 while.1
  360.7 19.7 %custom-call.16 = f32[2,128,128]{1,2,0:T(8,128)S(1)} custom-call(f32[2,128,128]{2,1,0:T(8,128)S(1)} %get-tuple-element.10), custom_call_target="InvertDiagBlocksLowerTriangular" | custom-call | tf_op jit(solution)/shard_map/jit(_solve_triangular)/triangular_solve | solution.py:36
  380.4 2.3 fusion.22
  382.7 3.0 convolution_subtract_fusion
  386.8 3.0 fusion.19
  395.0 24.7 %convolution_bitcast_fusion = f32[256,3,3584]{2,0,1:T(8,128)} fusion(bf16[3,2048,3584]{2,1,0:T(8,128)(2,1)} %param.6, bf16[3,2048,256]{2,1,0:T(8,128)(2,1)} %param.8, pred[3]{0:T(512)(128)(4,1)S(1)} %iota_compare_fusion.3, bf16[2048,256]{1,0:T(8,128)(2,1)S(1)} %copy.11), kind=kOutput, calls=%fused_computation.11 | convolution fusion | flops 11275862016 | bytes 59244548 | tf_op jit(solution)/shard_map/kdr,kdc->rkc/dot_general | solution.py:42
  419.8 13.3 %all-reduce.15.cloned.1.call-done = f32[256,256]{1,0:T(8,128)} async-done(((f32[256,256]{1,0:T(8,128)}), f32[256,256]{1,0:T(8,128)}) %all-reduce.15.cloned.1.call-update) | async-done | bytes 262160 | tf_op jit(solution)/shard_map/psum | solution.py:37
  433.0 4.4 fusion.9
  437.4 46.3 %all-gather.5.cloned.1.call-done = f32[1,256,3584]{2,1,0:T(8,128)} async-done(((f32[1,64,3584]{2,1,0:T(8,128)}), f32[1,256,3584]{2,1,0:T(8,128)}) %all-gather.5.cloned.1.call-update) | async-done | bytes 3670032 | tf_op jit(solution)/shard_map/all_gather | solution.py:53
  483.7 5.3 fusion.11
  489.0 105.6 %reduce-scatter.2.cloned.1.call-done = f32[64,3,3584]{2,0,1:T(8,128)} async-done(((f32[256,3,3584]{2,0,1:T(8,128)}), f32[64,3,3584]{2,0,1:T(8,128)}) %reduce-scatter.2.cloned.1.call-update) | async-done | bytes 2752528 | tf_op jit(solution)/shard_map/reduce_scatter | solution.py:41
  594.6 7.8 %divide_convert_fusion = (bf16[3,64,3584]{2,1,0:T(8,128)(2,1)}, f32[3,64,3584]{2,1,0:T(8,128)}, f32[3,64,3584]{2,1,0:T(8,128)}) fusion(f32[64,3,3584]{2,0,1:T(8,128)} %reduce-scatter.2.cloned.1.call-done, f32[3,64,3584]{2,1,0:T(8,128)} %param.10, f32[64,3584]{1,0:T(8,128)S(1)} %fusion.9, pred[3]{0:T(512)(128)(4,1)S(1)} %iota_compare_fusion.3, ...), kind=kLoop, calls=%fused_computation.23 | loop fusion | flops 8257536 | bytes 16973828 | tf_op jit(solution)/shard_map/convert_element_type | solution.py:63
  (45 shorter events, 15.2 us)
Async XLA Ops:
  7.2 1.5 copy-start
  7.2 78.1 %all-reduce.7.cloned.1.call-start = ((), (), s32[]{:S(2)}) async-start(), calls=%async_computation.1 | async-start | bytes 4194304 | tf_op jit(solution)/shard_map/psum | solution.py:27
  17.3 175.1 %all-reduce.9.cloned.1.call-start = ((), (), s32[]{:S(2)}) async-start(), calls=%async_computation.2 | async-start | bytes 7340032 | tf_op jit(solution)/shard_map/psum | solution.py:31
  96.9 172.2 %all-reduce.11.cloned.1.call-start = ((), (), s32[]{:S(2)}) async-start(), calls=%async_computation.3 | async-start | bytes 4194304 | tf_op jit(solution)/shard_map/psum | solution.py:32
  203.9 114.4 %all-reduce.13.cloned.1.call-start = ((), (), s32[]{:S(2)}) async-start(), calls=%async_computation.4 | async-start | bytes 524288 | tf_op jit(solution)/shard_map/psum | solution.py:34
  275.6 144.2 %all-gather.7.cloned.1.call-start = ((), (), s32[]{:S(2)}) async-start(), calls=%async_computation.8 | async-start | bytes 4587520 | tf_op jit(solution)/shard_map/all_gather | solution.py:54
  277.8 155.2 %all-reduce.15.cloned.1.call-start = ((), (), s32[]{:S(2)}) async-start(), calls=%async_computation.5 | async-start | bytes 524288 | tf_op jit(solution)/shard_map/psum | solution.py:37
  389.9 93.8 %all-gather.5.cloned.1.call-start = ((), (), s32[]{:S(2)}) async-start(), calls=%async_computation.7 | async-start | bytes 4587520 | tf_op jit(solution)/shard_map/all_gather | solution.py:53
  392.1 202.5 %reduce-scatter.2.cloned.1.call-start = ((), (), s32[]{:S(2)}) async-start(), calls=%async_computation.6 | async-start | bytes 13762560 | tf_op jit(solution)/shard_map/reduce_scatter | solution.py:41
  594.6 7.8 %copy-start.1 = (bf16[3584,256]{1,0:T(8,128)(2,1)S(1)}, bf16[3584,256]{1,0:T(8,128)(2,1)}, u32[]{:S(2)}) copy-start(bf16[3584,256]{1,0:T(8,128)(2,1)} %param.7) | copy-start | bytes 5505028
Sparse Core Ops, SparseCore 0:
  17.4 67.8 all-reduce.6
  97.0 95.2 all-reduce.8
  204.1 65.0 all-reduce.10
  275.7 42.6 all-reduce.12
  320.6 48.3 all-gather.6
  390.0 43.0 all-reduce.14
  435.5 48.1 all-gather.4
  486.8 107.7 reduce-scatter.1
where the time goes:
time: 617 us; the launch traced here: 609 us
  waiting for transfers between devices  434 us (70%)
  matrix products  82.4 us (13%)
  other arithmetic  63.6 us (10%)
  between operations  16.6 us (3%)
  local copies, waits for them, and re-layouts  11.9 us (2%)
    reduce_scatter x1, waiting for transfers between devices, local(): lax.psum_scatter(jnp.einsum('kdr,kdc->rkc', projectors, grads, preferred_...  106 us
    psum x1, waiting for transfers between devices, local(): lax.psum(backward_part, 'dp') / columns_total  95.4 us
    psum x1, waiting for transfers between devices, local(): sketched = (lax.psum(sketch_part, 'mp') / rank_total).astype(jnp.bfloat16)  68 us
    psum x1, waiting for transfers between devices, local(): lax.psum(jnp.dot(target, backward, preferred_element_type=jnp.float32), '...  64.7 us
    all_gather x1, waiting for transfers between devices, local(): lax.all_gather(first_own, 'dp', axis=0, tiled=True)  46.3 us
    psum x1, waiting for transfers between devices, local(): gram_full = lax.psum(gram_part, 'dp')  40.5 us
    another operation x6, other arithmetic, local(): factor = jnp.linalg.cholesky(gram_full)  34 us
    dot_general x1, matrix products, local(): jnp.einsum('kdr,kdc->rkc', projectors, grads, preferred_element_type=jnp....  24.7 us
  transfers between devices with their start and end apart: 8, of which 7 were waited for; matrix products, arithmetic and copies ran while one was open for 18% of the time, Pallas kernels for 0%

commit v1 on v0

--- a/solution.py
+++ b/solution.py
@@ -31,7 +31,11 @@
     backward = (lax.psum(backward_part, "dp") / columns_total).astype(jnp.bfloat16)
     range_panel = lax.psum(jnp.dot(target, backward, preferred_element_type=jnp.float32), "mp")
     gram_part = row_product(range_panel, range_panel)
-    gram_full = lax.psum(gram_part, "dp")
+    gram_full = gram_part
+    for hop in (1, 2):
+        gram_full = gram_full + lax.ppermute(
+            gram_full, "dp", [(dev, dev ^ hop) for dev in range(4)]
+        )
     factor = jnp.linalg.cholesky(gram_full)
     new_basis = jax.scipy.linalg.solve_triangular(factor, range_panel.T, lower=True).T
     turning = lax.psum(row_product(new_basis, prior_proj), "dp")

time: 617 us -> 591 us (0.958)
  waiting for transfers between devices: 434 us -> 408 us
    psum x1 -> x0, waiting for transfers between devices: 40.5 us -> none  [local(): gram_full = lax.psum(gram_part, 'dp')]
    ppermute x0 -> x2, waiting for transfers between devices: none -> 18.7 us  [local(): lax.ppermute(gram_full, 'dp', [(dev, dev ^ hop) for dev in range(4)])]
  transfers between devices with their start and end apart: 8 -> 9, of which waited for: 7 -> 8; matrix products, arithmetic and copies ran while one was open for 18% -> 20% of each run, Pallas kernels for 0% -> 0%
where the time goes in v1:
time: 591 us; the launch traced here: 583 us
  waiting for transfers between devices  408 us (69%)
  matrix products  81.5 us (14%)
  other arithmetic  62.9 us (11%)
  between operations  16.5 us (3%)
  local copies, waits for them, and re-layouts  10.6 us (2%)
    reduce_scatter x1, waiting for transfers between devices, local(): lax.psum_scatter(jnp.einsum('kdr,kdc->rkc', projectors, grads, preferred_...  106 us
    psum x1, waiting for transfers between devices, local(): lax.psum(backward_part, 'dp') / columns_total  95.4 us
    psum x1, waiting for transfers between devices, local(): sketched = (lax.psum(sketch_part, 'mp') / rank_total).astype(jnp.bfloat16)  68 us
    psum x1, waiting for transfers between devices, local(): lax.psum(jnp.dot(target, backward, preferred_element_type=jnp.float32), '...  62.5 us
    all_gather x1, waiting for transfers between devices, local(): lax.all_gather(first_own, 'dp', axis=0, tiled=True)  46.1 us
    another operation x6, other arithmetic, local(): factor = jnp.linalg.cholesky(gram_full)  34.2 us
    dot_general x1, matrix products, local(): jnp.einsum('kdr,kdc->rkc', projectors, grads, preferred_element_type=jnp....  24.6 us
    another operation x3, other arithmetic, local(): jax.scipy.linalg.solve_triangular(factor, range_panel.T, lower=True)  19.7 us
  transfers between devices with their start and end apart: 9, of which 8 were waited for; matrix products, arithmetic and copies ran while one was open for 20% of the time, Pallas kernels for 0%

profile of v1, /device:TPU:0, one launch (start us, length us, event | category | flops | bytes accessed | tf_op | source)
XLA Modules:
  0.0 583.2 jit_solution(1167710816651924543)
XLA Ops:
  8.7 8.6 %fusion.4 = f32[2048,256]{1,0:T(8,128)} fusion(bf16[3584,256]{1,0:T(8,128)(2,1)S(1)} %copy-done, bf16[3,2048,3584]{2,1,0:T(8,128)(2,1)} %param.6, s32[]{:T(128)S(6)} %select_n.27), kind=kOutput, calls=%fused_computation.6 | convolution fusion | flops 3758096384 | bytes 18612228 | tf_op jit(solution)/shard_map/dot_general | solution.py:26
  17.3 68.0 %all-reduce.6.cloned.1.call-done = f32[2048,256]{1,0:T(8,128)} async-done(((f32[2048,256]{1,0:T(8,128)}), f32[2048,256]{1,0:T(8,128)}) %all-reduce.6.cloned.1.call-update) | async-done | bytes 2097168 | tf_op jit(solution)/shard_map/psum | solution.py:27
  85.3 11.6 %fusion.2 = f32[3584,256]{1,0:T(8,128)} fusion(bf16[3,2048,3584]{2,1,0:T(8,128)(2,1)} %param.6, s32[]{:T(128)S(6)} %select_n.27, f32[2048,256]{1,0:T(8,128)} %all-reduce.6.cloned.1.call-done), kind=kOutput, calls=%fused_computation.4 | convolution fusion | flops 3759144960 | bytes 20447236 | tf_op jit(solution)/shard_map/dot_general | solution.py:28
  97.0 95.4 %all-reduce.8.cloned.1.call-done = f32[3584,256]{1,0:T(8,128)} async-done(((f32[3584,256]{1,0:T(8,128)}), f32[3584,256]{1,0:T(8,128)}) %all-reduce.8.cloned.1.call-update) | async-done | bytes 3670032 | tf_op jit(solution)/shard_map/psum | solution.py:31
  192.4 11.5 %fusion = f32[2048,256]{1,0:T(8,128)} fusion(bf16[3,2048,3584]{2,1,0:T(8,128)(2,1)} %param.6, s32[]{:T(128)S(6)} %select_n.27, f32[3584,256]{1,0:T(8,128)} %all-reduce.8.cloned.1.call-done), kind=kOutput, calls=%fused_computation.2 | convolution fusion | flops 3759931392 | bytes 20447236 | tf_op jit(solution)/shard_map/dot_general | solution.py:32
  206.7 62.5 %all-reduce.10.cloned.1.call-done = f32[2048,256]{1,0:T(8,128)} async-done(((f32[2048,256]{1,0:T(8,128)}), f32[2048,256]{1,0:T(8,128)}) %all-reduce.10.cloned.1.call-update) | async-done | bytes 2097168 | tf_op jit(solution)/shard_map/psum | solution.py:32
  269.2 5.7 fusion.48
  276.4 6.6 %collective-permute-done = f32[256,256]{0,1:T(8,128)S(1)} collective-permute-done((f32[256,256]{0,1:T(8,128)S(1)}, f32[256,256]{0,1:T(8,128)S(1)}, u32[]{:S(2)}, u32[]{:S(2)}) %collective-permute-start) | collective-permute-done | bytes 262176 | tf_op jit(solution)/shard_map/ppermute | solution.py:36
  284.0 12.1 %collective-permute-done.1 = f32[256,256]{0,1:T(8,128)S(1)} collective-permute-done((f32[256,256]{0,1:T(8,128)S(1)}, f32[256,256]{0,1:T(8,128)S(1)}, u32[]{:S(2)}, u32[]{:S(2)}) %collective-permute-start.1) | collective-permute-done | bytes 262176 | tf_op jit(solution)/shard_map/ppermute | solution.py:36
  296.3 11.7 %cholesky.50 = f32[128,128]{1,0:T(8,128)S(1)} custom-call(f32[128,128]{1,0:T(8,128)S(1)} %cholesky.118), custom_call_target="Cholesky" | custom-call | tf_op jit(solution)/shard_map/jit(cholesky)/cholesky | solution.py:39
  308.1 9.8 %custom-call.15 = f32[1,128,128]{1,2,0:T(8,128)S(1)} custom-call(f32[1,128,128]{2,1,0:T(8,128)S(1)} %get-tuple-element.27), custom_call_target="InvertDiagBlocksLowerTriangular" | custom-call | tf_op jit(solution)/shard_map/jit(cholesky)/cholesky | solution.py:39
  318.4 11.9 %cholesky.105 = f32[128,128]{1,0:T(8,128)S(1)} custom-call(f32[128,128]{1,0:T(8,128)S(1)} %slice_subtract_fusion), custom_call_target="Cholesky" | custom-call | tf_op jit(solution)/shard_map/jit(cholesky)/cholesky | solution.py:39
  332.4 3.9 while.1
  336.2 19.7 %custom-call.16 = f32[2,128,128]{1,2,0:T(8,128)S(1)} custom-call(f32[2,128,128]{2,1,0:T(8,128)S(1)} %get-tuple-element.10), custom_call_target="InvertDiagBlocksLowerTriangular" | custom-call | tf_op jit(solution)/shard_map/jit(_solve_triangular)/triangular_solve | solution.py:40
  355.9 2.3 fusion.22
  358.2 3.0 convolution_subtract_fusion
  362.3 3.0 fusion.19
  370.5 24.6 %convolution_bitcast_fusion = f32[256,3,3584]{2,0,1:T(8,128)} fusion(bf16[3,2048,3584]{2,1,0:T(8,128)(2,1)} %param.6, bf16[3,2048,256]{2,1,0:T(8,128)(2,1)} %param.8, pred[3]{0:T(512)(128)(4,1)S(1)} %iota_compare_fusion.3, bf16[2048,256]{1,0:T(8,128)(2,1)S(1)} %copy.12), kind=kOutput, calls=%fused_computation.11 | convolution fusion | flops 11275862016 | bytes 59244548 | tf_op jit(solution)/shard_map/kdr,kdc->rkc/dot_general | solution.py:46
  395.2 11.8 %all-reduce.12.cloned.1.call-done = f32[256,256]{1,0:T(8,128)} async-done(((f32[256,256]{1,0:T(8,128)}), f32[256,256]{1,0:T(8,128)}) %all-reduce.12.cloned.1.call-update) | async-done | bytes 262160 | tf_op jit(solution)/shard_map/psum | solution.py:41
  406.9 4.4 fusion.9
  411.3 46.1 %all-gather.5.cloned.1.call-done = f32[1,256,3584]{2,1,0:T(8,128)} async-done(((f32[1,64,3584]{2,1,0:T(8,128)}), f32[1,256,3584]{2,1,0:T(8,128)}) %all-gather.5.cloned.1.call-update) | async-done | bytes 3670032 | tf_op jit(solution)/shard_map/all_gather | solution.py:57
  457.5 5.3 fusion.11
  462.8 105.6 %reduce-scatter.2.cloned.1.call-done = f32[64,3,3584]{2,0,1:T(8,128)} async-done(((f32[256,3,3584]{2,0,1:T(8,128)}), f32[64,3,3584]{2,0,1:T(8,128)}) %reduce-scatter.2.cloned.1.call-update) | async-done | bytes 2752528 | tf_op jit(solution)/shard_map/reduce_scatter | solution.py:45
  568.4 7.8 %divide_convert_fusion = (bf16[3,64,3584]{2,1,0:T(8,128)(2,1)}, f32[3,64,3584]{2,1,0:T(8,128)}, f32[3,64,3584]{2,1,0:T(8,128)}) fusion(f32[64,3,3584]{2,0,1:T(8,128)} %reduce-scatter.2.cloned.1.call-done, f32[3,64,3584]{2,1,0:T(8,128)} %param.10, f32[64,3584]{1,0:T(8,128)S(1)} %fusion.9, pred[3]{0:T(512)(128)(4,1)S(1)} %iota_compare_fusion.3, ...), kind=kLoop, calls=%fused_computation.23 | loop fusion | flops 8257536 | bytes 16973828 | tf_op jit(solution)/shard_map/convert_element_type | solution.py:67
  (48 shorter events, 17.8 us)
Async XLA Ops:
  7.2 1.5 copy-start
  7.2 78.1 %all-reduce.6.cloned.1.call-start = ((), (), s32[]{:S(2)}) async-start(), calls=%async_computation.1 | async-start | bytes 4194304 | tf_op jit(solution)/shard_map/psum | solution.py:27
  17.3 175.1 %all-reduce.8.cloned.1.call-start = ((), (), s32[]{:S(2)}) async-start(), calls=%async_computation.2 | async-start | bytes 7340032 | tf_op jit(solution)/shard_map/psum | solution.py:31
  96.9 172.2 %all-reduce.10.cloned.1.call-start = ((), (), s32[]{:S(2)}) async-start(), calls=%async_computation.3 | async-start | bytes 4194304 | tf_op jit(solution)/shard_map/psum | solution.py:32
  203.9 191.2 %all-gather.7.cloned.1.call-start = ((), (), s32[]{:S(2)}) async-start(), calls=%async_computation.7 | async-start | bytes 4587520 | tf_op jit(solution)/shard_map/all_gather | solution.py:58
  206.2 200.8 %all-reduce.12.cloned.1.call-start = ((), (), s32[]{:S(2)}) async-start(), calls=%async_computation.4 | async-start | bytes 524288 | tf_op jit(solution)/shard_map/psum | solution.py:41
  274.9 8.1 %collective-permute-start = (f32[256,256]{0,1:T(8,128)S(1)}, f32[256,256]{0,1:T(8,128)S(1)}, u32[]{:S(2)}, u32[]{:S(2)}) collective-permute-start(f32[256,256]{0,1:T(8,128)S(1)} %fusion.48), channel_id=1, source_target_pairs={{0,8},{8,0},{16,24},{24,16},{1,9},{9,1},{17,25},{25,17},{2,10},{10... | collective-permute-start | bytes 786440 | tf_op jit(solution)/shard_map/ppermute | solution.py:36
  283.0 13.1 %collective-permute-start.1 = (f32[256,256]{0,1:T(8,128)S(1)}, f32[256,256]{0,1:T(8,128)S(1)}, u32[]{:S(2)}, u32[]{:S(2)}) collective-permute-start(f32[256,256]{0,1:T(8,128)S(1)} %add.64), channel_id=1, source_target_pairs={{0,16},{8,24},{16,0},{24,8},{1,17},{9,25},{17,1},{25,9},{2,18},{10... | collective-permute-start | bytes 786440 | tf_op jit(solution)/shard_map/ppermute | solution.py:36
  365.4 92.1 %all-gather.5.cloned.1.call-start = ((), (), s32[]{:S(2)}) async-start(), calls=%async_computation.6 | async-start | bytes 4587520 | tf_op jit(solution)/shard_map/all_gather | solution.py:57
  367.6 200.7 %reduce-scatter.2.cloned.1.call-start = ((), (), s32[]{:S(2)}) async-start(), calls=%async_computation.5 | async-start | bytes 13762560 | tf_op jit(solution)/shard_map/reduce_scatter | solution.py:45
  568.4 7.8 %copy-start.1 = (bf16[3584,256]{1,0:T(8,128)(2,1)S(1)}, bf16[3584,256]{1,0:T(8,128)(2,1)}, u32[]{:S(2)}) copy-start(bf16[3584,256]{1,0:T(8,128)(2,1)} %param.7) | copy-start | bytes 5505028
Sparse Core Ops, SparseCore 0:
  17.4 67.8 all-reduce.5
  97.1 95.2 all-reduce.7
  204.1 65.0 all-reduce.9
  271.5 52.0 all-gather.6
  365.5 41.3 all-reduce.11
  409.2 48.1 all-gather.4
  460.6 107.7 reduce-scatter.1
